TPU v7x, 32 devices: a whole 2x2x4 slice. The times are simulated.
32 devices in a mesh: shot: 4 (over y, x), gx: 2 (over core), gy: 4 (over z).
Axes of the slice: x: 2, y: 2, z: 4, core: 2. Of those that a mesh axis runs over, the one named last changes fastest.
Arguments:
- fwd_now: float32 [8, 32, 128, 256], P('shot', 'gx', 'gy'), may hold values from -6 to 6
- fwd_next: float32 [8, 32, 128, 256], P('shot', 'gx', 'gy'), may hold values from -6 to 6
- adj_now: float32 [8, 32, 128, 256], P('shot', 'gx', 'gy'), may hold values from -6 to 6
- adj_next: float32 [8, 32, 128, 256], P('shot', 'gx', 'gy'), may hold values from -6 to 6
- courant: float32 [32, 128, 256], P('gx', 'gy'), may hold values from 0.15 to 0.45
- wavelet: float32 [8, 128], P('shot'), may hold values from -24 to 24
- traces: float32 [8, 128, 1024], P('shot'), may hold values from -6 to 6
- src_cells: int32 [8], P('shot'), may hold values from 0 to 4095
- rec_cells: int32 [8, 1024], P('shot'), may hold values from 0 to 4095
- step_index: int32 [8], P('shot'), may hold values from 1 to 127
Outputs:
- forward_prior: float32 [8, 32, 128, 256], P('shot', 'gx', 'gy')
- forward_start: float32 [8, 32, 128, 256], P('shot', 'gx', 'gy')
- adjoint_prior: float32 [8, 32, 128, 256], P('shot', 'gx', 'gy')
- adjoint_start: float32 [8, 32, 128, 256], P('shot', 'gx', 'gy')
- gradient: float32 [32, 128, 256], P('gx', 'gy', 'shot')
Inputs may be any that keep to these rules, and one draw needn't show every extreme that they name: `src_cells`: a horizontal cell x * 128 + y of the grid. `rec_cells`: a horizontal cell x * 128 + y of the grid; several receivers may share a cell. `step_index`: a time step k such that the samples k and k - 1 exist (k ≥ 1).
All inputs are finite; a program needn't handle non-finite values.
Results may differ from a plain program's by a relative error of at most 0.0003.
Values sent between devices are 32-bit elements; how exact they have to be, the bound alone decides.
No kernel may reach another device: no remote copies, remote signals or barrier semaphores. Data moves between devices by JAX's collectives and lax.ppermute only.
A program may use at most 64 MiB of HBM per device.

v0:
```python
import functools

import jax
import jax.numpy as jnp
from jax import lax
from jax.experimental import pallas as pl
from jax.experimental.pallas import tpu as pltpu
from jax.sharding import PartitionSpec as P


STEPS = 2
SRC_DEPTH = 4
REC_DEPTH = 6
COEFS = (-205.0 / 72.0, 8.0 / 5.0, -1.0 / 5.0, 8.0 / 315.0, -1.0 / 560.0)
F32 = jnp.float32
BF16 = jnp.bfloat16
VMEM = pl.BlockSpec(memory_space=pltpu.VMEM)
SMEM = pl.BlockSpec(memory_space=pltpu.SMEM)
HBM = pl.BlockSpec(memory_space=pltpu.HBM)


def iota(dim):
    return lax.broadcasted_iota(jnp.int32, (8, 128), dim)


def even_on(axis):
    return lax.axis_index(axis) % 2 == 0


def pair_permutes(axis, other):
    count, across = lax.axis_size(axis), lax.axis_size(other)
    perms = []

    def at(i, j):
        return i * across + j if axis == "gx" else j * count + i

    for first in (0, 1):
        pairs = [(i, i + 1) for i in range(first, count - 1, 2)]
        if not pairs:
            continue
        left = set(range(count)) - {i for pair in pairs for i in pair}
        perm = [(at(a, j), at(b, j)) for a, b in pairs for j in range(across)]
        perm += [(b, a) for a, b in perm]
        if across % 2 == 0:
            perm += [(at(i, j), at(i, j ^ 1)) for i in sorted(left) for j in range(across)]
        perms.append(perm)
    return perms


def has_neighbour(axis, step):
    at = lax.axis_index(axis) + step
    return (at >= 0) & (at < lax.axis_size(axis))


def edge_layer(axis, width, turn, k):
    high = even_on(axis) if turn == 0 else jnp.logical_not(even_on(axis))
    return jnp.where(high, width - 1 - k, k)


def in_hbm(x):
    return pltpu.with_memory_space_constraint(x, pltpu.HBM)


def in_vmem(x):
    return pltpu.with_memory_space_constraint(x, pltpu.VMEM)


def halves(depth):
    return [slice(h * 128, h * 128 + 128) for h in range(depth // 128)]


def write_y_sends(sends, at, x, z, low_0, low_1, high_0, high_1):
    sub = iota(0)
    low = jnp.where(sub < 4, low_0, pltpu.roll(low_1, 4, 0))
    high = jnp.where(sub < 4, pltpu.roll(high_0, 4, 0), high_1)
    even = even_on("gy")
    for turn, ref in enumerate(sends):
        pick = even if turn == 0 else jnp.logical_not(even)
        ref[at, x, :, z] = jnp.where(pick, high, low)


class Copies:
    def __init__(self, sems):
        self.sems, self.count = sems, 0

    def start(self, src, dst):
        copy = pltpu.make_async_copy(src, dst, self.sems.at[self.count])
        copy.start()
        self.count += 1
        return copy


def first_y_sends(u_hbm, a_hbm, c_hbm, *refs):
    *ys, u_low, u_high, a_low, a_high, c_low, c_high, sems = refs
    _, width_x, width_y, depth = u_hbm.shape
    copies = Copies(sems)
    waits = []
    for src, low, high in ((u_hbm, u_low, u_high), (a_hbm, a_low, a_high)):
        waits.append(copies.start(src.at[:, :, 0:8, :], low))
        waits.append(copies.start(src.at[:, :, width_y - 8 : width_y, :], high))
    waits.append(copies.start(c_hbm.at[:, 0:8, :], c_low))
    waits.append(copies.start(c_hbm.at[:, width_y - 8 : width_y, :], c_high))
    for wait in waits:
        wait.wait()

    def line(x, carry):
        for z in halves(depth):
            low = c_low[x, :, z] * c_low[x, :, z]
            high = c_high[x, :, z] * c_high[x, :, z]
            write_y_sends(ys, 0, x, z, *(ref[s, x, :, z] for ref in (u_low, u_high) for s in range(2)))
            write_y_sends(
                ys,
                1,
                x,
                z,
                *(m * ref[s, x, :, z] for m, ref in ((low, a_low), (high, a_high)) for s in range(2)),
            )
        return carry

    lax.fori_loop(0, width_x, line, 0, unroll=4)


def first_x_sends(u, a, cour, *xs):
    shots, width_x = u.shape[:2]
    for turn, ref in enumerate(xs):
        for k in range(4):
            x = edge_layer("gx", width_x, turn, k)
            for s in range(shots):
                ref[0, s, k] = u[s, x]
                ref[1, s, k] = cour[x] * cour[x] * a[s, x]


def band_of(apart):
    band = jnp.zeros(apart.shape, F32)
    for r in range(1, 5):
        band = jnp.where(apart == r, float(round(5040 * COEFS[r])), band)
    return band.astype(BF16)


def make_bands(band_y, band_z):
    rows, columns = band_y.shape
    at = lax.broadcasted_iota(jnp.int32, (rows, columns), 1) % rows
    band_y[...] = band_of(jnp.abs(at - lax.broadcasted_iota(jnp.int32, (rows, columns), 0)))
    depth = band_z.shape[1]
    at = lax.broadcasted_iota(jnp.int32, (depth, depth), 0)
    band = band_of(jnp.abs(at - lax.broadcasted_iota(jnp.int32, (depth, depth), 1)))
    for part in range(3):
        band_z[part * depth : part * depth + depth, :] = band


def three_parts(v):
    top = v.astype(BF16)
    rest = v - top.astype(F32)
    middle = rest.astype(BF16)
    return top, middle, (rest - middle.astype(F32)).astype(BF16)


BATCH = 8


def plane_stencil(block_of, shots, band_y, band_z, split, flat):
    depth = band_z.shape[1]
    width_y = band_y.shape[0]

    def layers(batch, carry):
        along_y = []
        for k in range(BATCH):
            for s in range(shots):
                parts = three_parts(block_of(s, BATCH * batch + k))
                rows = (k * shots + s) * width_y
                for part, value in enumerate(parts):
                    split[rows : rows + width_y, part * depth : part * depth + depth] = value
                stacked = jnp.concatenate(parts, axis=0)
                along_y.append(jnp.dot(band_y[...], stacked, preferred_element_type=F32))
        along_z = jnp.dot(split[...], band_z[...], preferred_element_type=F32)
        for k in range(BATCH):
            for s in range(shots):
                rows = (k * shots + s) * width_y
                both = along_z[rows : rows + width_y, :] + along_y[k * shots + s]
                flat[s, BATCH * batch + k] = both * (1.0 / 5040.0)
        return carry

    lax.fori_loop(0, flat.shape[1] // BATCH, layers, 0)


def laplace_line(field, flat, s, row, z):
    width_x = flat.shape[1]
    line = [field[s, x, row, z] for x in range(width_x)]
    for x in range(width_x):
        total = 3.0 * COEFS[0] * line[x] + flat[s, x, row, z]
        for r in range(1, 5):
            near = [line[i] for i in (x - r, x + r) if 0 <= i < width_x]
            if near:
                total = total + COEFS[r] * (near[0] if len(near) == 1 else near[0] + near[1])
        yield x, line[x], total


def place(cells, rows_y, width_x, width_y):
    bits = rows_y.bit_length() - 1
    x = lax.shift_right_logical(cells, bits) - lax.axis_index("gx") * width_x
    y = (cells & (rows_y - 1)) - lax.axis_index("gy") * width_y
    return x, y


def forward_march(offset, rows_y, step_ref, src_ref, wave_ref, u, u_old, a, cour, *refs):
    if offset:
        band_y, band_z, image_in, u_out, image, prior, *refs = refs
    else:
        u_out, image, band_y, band_z, *refs = refs
    split, flat, *old, sems = refs
    shots, width_x, width_y, depth = u.shape
    copies = Copies(sems)
    moves = [copies.start(u, prior) if offset else copies.start(u_old, old[0])]
    u_old = u_old if offset else old[0]
    if not offset:
        make_bands(band_y, band_z)
    plane_stencil(lambda s, x: u[s, x], shots, band_y, band_z, split, flat)
    if not offset:
        moves.pop().wait()

    def tiles(t, carry):
        row = pl.ds(pl.multiple_of(8 * t, 8), 8)
        for h, z in enumerate(halves(depth)):
            for s in range(shots):
                for x, center, lap in laplace_line(u, flat, s, row, z):
                    mass = cour[x, row, z] * cour[x, row, z]
                    u_out[s, x, row, z] = 2.0 * center - u_old[s, x, row, z] + mass * lap
                    term = a[s, x, row, z] * lap
                    if s:
                        image[h, x, row, :] = image[h, x, row, :] + term
                    else:
                        image[h, x, row, :] = image_in[h, x, row, :] + term if offset else term
        return carry

    lax.fori_loop(0, width_y // 8, tiles, 0)
    lane, sub = iota(1), iota(0)
    for s in range(shots):
        at_x, at_y = place(src_ref[s], rows_y, width_x, width_y)

        @pl.when((at_x >= 0) & (at_x < width_x) & (at_y >= 0) & (at_y < width_y))
        def _():
            row = pl.ds(pl.multiple_of((at_y // 8) * 8, 8), 8)
            speed = cour[at_x, row, 0:128]
            hit = (sub == at_y % 8) & (lane == SRC_DEPTH)
            added = jnp.where(hit, speed * speed * wave_ref[s, step_ref[s] - offset], 0.0)
            u_out[s, at_x, row, 0:128] = u_out[s, at_x, row, 0:128] + added

    for move in moves:
        move.wait()


def adjoint_march(offset, rows_y, step_ref, rec_hbm, trace_hbm, a, a_old, cour, band_y, band_z, *refs):
    done, refs = (refs[0], refs[1:]) if offset else (None, refs)
    a_out, *refs = refs
    outs, refs = (refs[:2], refs[2:]) if offset else ((), refs)
    split, flat, scaled, trace, rec_ref, *old, sems = refs
    shots, width_x, width_y, depth = a.shape
    copies = Copies(sems)
    loads = [copies.start(rec_hbm, rec_ref)]
    for s in range(shots):
        block = pl.multiple_of(((step_ref[s] - offset) // 8) * 8, 8)
        loads.append(copies.start(trace_hbm.at[s, pl.ds(block, 8), :], trace.at[s]))
    if offset:
        moves = [copies.start(src, dst) for src, dst in zip((a, done), outs)]
    else:
        moves = [copies.start(a_old, old[0])]
        a_old = old[0]

    def scale(s, x):
        block = cour[x] * cour[x] * a[s, x]
        scaled[s, x] = block
        return block

    plane_stencil(scale, shots, band_y, band_z, split, flat)
    if not offset:
        moves.pop().wait()

    def tiles(t, carry):
        row = pl.ds(pl.multiple_of(8 * t, 8), 8)
        for z in halves(depth):
            for s in range(shots):
                for x, _, lap in laplace_line(scaled, flat, s, row, z):
                    a_out[s, x, row, z] = 2.0 * a[s, x, row, z] - a_old[s, x, row, z] + lap
        return carry

    lax.fori_loop(0, width_y // 8, tiles, 0)
    for load in loads:
        load.wait()
    for s in range(shots):
        moment = step_ref[s] - offset
        pick = lax.broadcasted_iota(jnp.int32, trace.shape[1:], 0) == moment % 8
        values = jnp.sum(jnp.where(pick, trace[s], 0.0), axis=0, keepdims=True)
        at_x, at_y = place(rec_ref[s : s + 1, :], rows_y, width_x, width_y)
        count = at_x.shape[1]
        hot_x = lax.broadcasted_iota(jnp.int32, (width_x, count), 0) == at_x
        hot_y = lax.broadcasted_iota(jnp.int32, (width_y, count), 0) == at_y
        spread = [jnp.where(hot_y, part.astype(F32), 0.0).astype(BF16) for part in three_parts(values)]
        planes = lax.dot_general(
            jnp.concatenate(spread, axis=0),
            jnp.where(hot_x, 1.0, 0.0).astype(BF16),
            (((1,), (1,)), ((), ())),
            preferred_element_type=F32,
        )
        plane = planes[0:width_y] + planes[width_y : 2 * width_y] + planes[2 * width_y :]
        depth_mask = lax.broadcasted_iota(jnp.int32, (width_y, 128), 1) == REC_DEPTH
        for x in range(width_x):
            added = jnp.where(depth_mask, plane[:, x : x + 1], 0.0)
            a_out[s, x, :, 0:128] = a_out[s, x, :, 0:128] + added
    for move in moves:
        move.wait()


def packed(load, target, x):
    lane = lax.broadcasted_iota(jnp.int32, (16, 128), 1)
    block = load(target // 2, x)
    top, bottom = block[0:16, :], block[16:32, :]
    front = jnp.where(lane < 64, top, pltpu.roll(bottom, 64, 1))
    back = jnp.where(lane < 64, pltpu.roll(top, 64, 1), bottom)
    return jnp.where(target % 2 == 0, front, back)


def add_edges(hy, hx, field_at, out, cour, forward, a, image):
    shots, width_x, width_y, depth = out.shape
    sub = iota(0)
    even = even_on("gy")
    has_below, has_above = has_neighbour("gy", -1), has_neighbour("gy", 1)

    def coef(values):
        row = jnp.zeros((8, 128), F32)
        for j, v in values:
            row = jnp.where(sub == j, v, row)
        return row

    low_coef = [None] + [coef([(j, COEFS[r]) for j in range(4) if j < r]) for r in range(1, 5)]
    high_coef = [None] + [coef([(p, COEFS[r]) for p in range(4, 8) if p >= 8 - r]) for r in range(1, 5)]

    def turned(v, shift):
        return v if shift % 8 == 0 else pltpu.roll(v, shift % 8, 0)

    def rows(x, carry):
        for h, z in enumerate(halves(depth)):
            first = hy[0][field_at, x, :, z]
            second = hy[1][field_at, x, :, z] if len(hy) > 1 else jnp.zeros_like(first)
            below = jnp.where(has_below, jnp.where(even, second, first), 0.0)
            above = jnp.where(has_above, jnp.where(even, first, second), 0.0)
            for side in range(2):
                row = slice(0, 8) if side == 0 else slice(width_y - 8, width_y)
                for s in range(shots):
                    lap = None
                    for r in range(1, 5):
                        if side == 0:
                            part = low_coef[r] * turned(below, r - 4 + 4 * s)
                        else:
                            part = high_coef[r] * turned(above, 8 - r - 4 * s)
                        lap = part if lap is None else lap + part
                    if forward:
                        mass = cour[x, row, z] * cour[x, row, z]
                        out[s, x, row, z] = out[s, x, row, z] + mass * lap
                        image[h, x, row, :] = image[h, x, row, :] + a[s, x, row, z] * lap
                    else:
                        out[s, x, row, z] = out[s, x, row, z] + lap
        return carry

    lax.fori_loop(0, width_x, rows, 0, unroll=4)
    for turn, ref in enumerate(hx):
        toward = jnp.where(even_on("gx"), 1, -1) * (1 if turn == 0 else -1)
        whole = turn == 0 and lax.axis_size("gx") % 2 == 0
        for j in range(4):
            x = edge_layer("gx", width_x, turn, j)
            for h, z in enumerate(halves(depth)):
                for s in range(shots):
                    lap = None
                    for k in range(4 - j):
                        part = COEFS[j + k + 1] * ref[field_at, s, k, :, z]
                        lap = part if lap is None else lap + part
                    if not whole:
                        lap = jnp.where(has_neighbour("gx", toward), lap, 0.0)
                    if forward:
                        mass = cour[x, :, z] * cour[x, :, z]
                        out[s, x, :, z] = out[s, x, :, z] + mass * lap
                        image[h, x] = image[h, x] + a[s, x, :, z] * lap
                    else:
                        out[s, x, :, z] = out[s, x, :, z] + lap


def write_sends(turns_y, sends, out, cour):
    shots, width_x, width_y, depth = out.shape
    ys, xs = sends[:turns_y], sends[turns_y:]

    def line(x, carry):
        for z in halves(depth):
            tiles = []
            for row in (slice(0, 8), slice(width_y - 8, width_y)):
                for s in range(shots):
                    tile = out[s, x, row, z]
                    tiles.append(tile if cour is None else cour[x, row, z] * cour[x, row, z] * tile)
            write_y_sends(ys, 0, x, z, *tiles)
        return carry

    lax.fori_loop(0, width_x, line, 0, unroll=4)
    for turn, ref in enumerate(xs):
        for k in range(4):
            x = edge_layer("gx", width_x, turn, k)
            for s in range(shots):
                ref[0, s, k] = out[s, x] if cour is None else cour[x] * cour[x] * out[s, x]


def forward_edge(turns_x, turns_y, last, *refs):
    hy, hx, refs = refs[:turns_y], refs[turns_y : turns_y + turns_x], refs[turns_y + turns_x :]
    a, cour, *refs = refs
    u_out, image, *sends = refs[2 if last else 3 :]
    add_edges(hy, hx, 0, u_out, cour, True, a, image)
    if not last:
        write_sends(turns_y, sends, u_out, None)
        return
    me = lax.axis_index("shot")
    lane = lax.broadcasted_iota(jnp.int32, (16, 128), 1)

    def parts(x, carry):
        pairs = []
        for h in range(2):
            top, bottom = image[h, x, 0:16, :], image[h, x, 16:32, :]
            front = jnp.where(lane < 64, top, pltpu.roll(bottom, 64, 1))
            back = jnp.where(lane < 64, pltpu.roll(top, 64, 1), bottom)
            odd = me % 2 == 1
            pairs.append((jnp.where(odd, back, front), jnp.where(odd, front, back)))
        for k, ref in enumerate(sends):
            ref[x] = jnp.where(me // 2 == 1, pairs[1 - k // 2][k % 2], pairs[k // 2][k % 2])
        return carry

    lax.fori_loop(0, u_out.shape[1], parts, 0, unroll=4)


def adjoint_edge(turns_x, turns_y, field_at, last, *refs):
    hy, hx, refs = refs[:turns_y], refs[turns_y : turns_y + turns_x], refs[turns_y + turns_x :]
    cour, _, a_out, *refs = refs
    add_edges(hy, hx, field_at, a_out, cour, False, None, None)
    if not last:
        write_sends(turns_y, refs, a_out, cour)
        return
    final, sem = refs
    copy = pltpu.make_async_copy(a_out, final, sem.at[0])
    copy.start()
    copy.wait()


def finish(scale, cour, own, first, second, third, out):
    me = lax.axis_index("shot")

    def line(x, carry):
        speed = packed(lambda h, x: jnp.where(h == 0, cour[x, :, 0:128], cour[x, :, 128:256]), me, x)
        total = own[x] + first[x] + second[x] + third[x]
        value = 2.0 * speed * total / scale
        out[x, 0:16, :] = value[:, 0:64]
        out[x, 16:32, :] = value[:, 64:128]
        return carry

    lax.fori_loop(0, out.shape[0], line, 0, unroll=4)


def call(body, outs, scratch, in_specs, args, cost, aliases=None, out_specs=None, limit=24 << 20):
    return pl.pallas_call(
        body,
        out_shape=outs,
        in_specs=in_specs,
        out_specs=out_specs or [VMEM] * len(outs),
        scratch_shapes=scratch,
        input_output_aliases=aliases or {},
        compiler_params=pltpu.CompilerParams(vmem_limit_bytes=limit),
        cost_estimate=pl.CostEstimate(flops=cost, bytes_accessed=cost, transcendentals=0),
    )(*args)


def shards(
    fwd_now, fwd_next, adj_now, adj_next, courant, wavelet, traces, src_cells, rec_cells, step_index
):
    shots, width_x, width_y, depth = fwd_now.shape
    groups = lax.axis_size("shot")
    rows_y = width_y * lax.axis_size("gy")
    assert rows_y & (rows_y - 1) == 0 and depth == 256 and groups == 4 and width_y == 32 and shots == 2
    perms_x, perms_y = pair_permutes("gx", "gy"), pair_permutes("gy", "gx")
    turns_x, turns_y = len(perms_x), len(perms_y)

    def shape(*dims):
        return jax.ShapeDtypeStruct(dims, F32)

    def swap(sends, perms):
        halos = []
        for send, perm in zip(sends, perms):
            halos.append(lax.ppermute(send, ("gx", "gy"), perm))
        return halos

    wave = shape(*fwd_now.shape)
    strip = shape(2, width_x, width_y, 128)
    y_send, x_rows = (width_x, 8, depth), (shots, 4, width_y, depth)
    y_rows = (shots, width_x, 8, depth)
    first_y = call(
        first_y_sends,
        [shape(2, *y_send)] * turns_y,
        [pltpu.VMEM(y_rows, F32)] * 4 + [pltpu.VMEM(y_rows[1:], F32)] * 2 + [pltpu.SemaphoreType.DMA((6,))],
        [HBM] * 3,
        (in_hbm(fwd_now), in_hbm(adj_now), in_hbm(courant)),
        1 << 20,
    )
    hy_u = hy_a = swap(first_y, perms_y)
    first_x = call(
        first_x_sends,
        [shape(2, *x_rows)] * turns_x,
        [],
        [VMEM] * 3,
        (fwd_now, adj_now, courant),
        1 << 20,
    )
    hx_u = hx_a = swap(first_x, perms_x)
    next_sends = [shape(1, *y_send)] * turns_y + [shape(1, *x_rows)] * turns_x
    bands = [jax.ShapeDtypeStruct((width_y, 3 * width_y), BF16), jax.ShapeDtypeStruct((3 * depth, depth), BF16)]
    stencil = [
        pltpu.VMEM((BATCH * shots * width_y, 3 * depth), BF16),
        pltpu.VMEM(fwd_now.shape, F32),
    ]
    sample = [pltpu.VMEM((shots, 8, traces.shape[-1]), F32), pltpu.VMEM(rec_cells.shape, jnp.int32)]
    u_now, u_next, a_now, a_next = fwd_now, fwd_next, adj_now, adj_next
    image = None
    for offset in range(STEPS):
        last = offset == STEPS - 1
        old_spec = VMEM if offset else HBM
        old_rows = [] if offset else [pltpu.VMEM(fwd_now.shape, F32)]
        old = u_next if offset else in_hbm(u_next)
        u_prev, image, *rest = call(
            functools.partial(forward_march, offset, rows_y),
            [wave, strip] + ([wave] if offset else bands),
            stencil + old_rows + [pltpu.SemaphoreType.DMA((1,))],
            [SMEM] * 3 + [VMEM, old_spec] + [VMEM] * (2 + 3 * offset),
            (step_index, src_cells, wavelet, u_now, old, a_now, courant) + ((*bands, image) if offset else ()),
            8 << 20,
            out_specs=[VMEM] * 2 + ([HBM] if offset else [VMEM] * 2),
        )
        if offset:
            forward_prior = rest[0]
        else:
            bands = rest

        def run_forward_edge(u_prev, image, *after):
            args = (*hy_u, *hx_u, a_now, courant, *after, in_vmem(u_prev), in_vmem(image))
            return call(
                functools.partial(forward_edge, turns_x, turns_y, last),
                [wave, strip] + ([shape(width_x, 16, 128)] * groups if last else next_sends),
                [],
                [VMEM] * len(args),
                args,
                1 << 20,
                {len(args) - 2: 0, len(args) - 1: 1},
            )

        def run_adjoint_march(*done):
            old = a_next if offset else in_hbm(a_next)
            return call(
                functools.partial(adjoint_march, offset, rows_y),
                [wave] * (1 + 2 * offset),
                stencil + stencil[1:] + sample + old_rows + [pltpu.SemaphoreType.DMA((shots + 3,))],
                [SMEM] + [HBM] * 2 + [VMEM, old_spec] + [VMEM] * (3 + offset),
                (step_index, in_hbm(rec_cells), in_hbm(traces), a_now, old, courant, *bands)
                + tuple(in_vmem(d) for d in done),
                8 << 20,
                out_specs=[VMEM] + [HBM] * (2 * offset),
            )

        if offset:
            u_prev, image, *u_sends = run_forward_edge(u_prev, image)
            a_prev, *rest = run_adjoint_march(u_prev)
        else:
            a_prev, *rest = run_adjoint_march()
            u_prev, image, *u_sends = run_forward_edge(u_prev, image, a_prev)
        if last:
            parts = [u_sends[0]]
            for k in (3, 1, 2):
                parts.append(lax.ppermute(u_sends[k], "shot", [(i, i ^ k) for i in range(groups)]))
        else:
            hy_u = swap(u_sends[:turns_y], perms_y)
            hx_u = swap(u_sends[turns_y:], perms_x)
        if offset:
            adjoint_prior, forward_start = rest
        args = (*hy_a, *hx_a, courant, in_vmem(a_prev))
        a_prev, *a_sends = call(
            functools.partial(adjoint_edge, turns_x, turns_y, 0 if offset else 1, last),
            [wave] + ([wave] if last else next_sends),
            [pltpu.SemaphoreType.DMA((1,))] if last else [],
            [VMEM] * len(args),
            args,
            1 << 20,
            {len(args) - 1: 0},
            out_specs=[VMEM, HBM] if last else None,
        )
        if last:
            (adjoint_start,) = a_sends
        else:
            hy_a = swap(a_sends[:turns_y], perms_y)
            hx_a = swap(a_sends[turns_y:], perms_x)
        u_next, u_now = u_now, u_prev
        a_next, a_now = a_now, a_prev
    (gradient,) = call(
        functools.partial(finish, float(shots * groups * STEPS)),
        [shape(width_x, width_y, depth // groups)],
        [],
        [VMEM] * 5,
        (courant, *parts),
        1 << 20,
    )
    return (forward_prior, forward_start, adjoint_prior, adjoint_start, gradient)


def solution(mesh):
    fields = P("shot", "gx", "gy", None)
    in_specs = (fields,) * 4 + (
        P("gx", "gy", None),
        P("shot", None),
        P("shot", None, None),
        P("shot"),
        P("shot", None),
        P("shot"),
    )
    out_specs = (fields,) * 4 + (P("gx", "gy", "shot"),)
    return jax.shard_map(shards, mesh=mesh, in_specs=in_specs, out_specs=out_specs, check_vma=False)
```

profile of v0, /device:TPU:0, one launch (start us, length us, event | category | flops | bytes accessed | tf_op | source)
XLA Modules:
  0.0 36.3 jit_solution(1180960959870790877)
XLA Ops:
  0.6 0.0 copy-start
  0.6 1.0 %copy-done = f32[16,32,256]{2,1,0:T(8,128)S(1)} copy-done((f32[16,32,256]{2,1,0:T(8,128)S(1)}, f32[16,32,256]{2,1,0:T(8,128)}, u32[]{:S(2)}) %copy-start) | copy-done | bytes 524312
  1.7 1.2 %copy-done.2 = f32[2,16,32,256]{3,2,1,0:T(8,128)S(1)} copy-done((f32[2,16,32,256]{3,2,1,0:T(8,128)S(1)}, f32[2,16,32,256]{3,2,1,0:T(8,128)}, u32[]{:S(2)}) %copy-start.2) | copy-done | bytes 1048600
  2.9 1.2 %copy-done.4 = f32[2,16,32,256]{3,2,1,0:T(8,128)S(1)} copy-done((f32[2,16,32,256]{3,2,1,0:T(8,128)S(1)}, f32[2,16,32,256]{3,2,1,0:T(8,128)}, u32[]{:S(2)}) %copy-start.4) | copy-done | bytes 1048600
  4.2 0.0 copy-start.3
  4.2 0.0 copy-start.5
  4.2 0.6 %collective-permute-start.2 = (f32[2,2,4,32,256]{4,3,2,1,0:T(8,128)S(1)}, f32[2,2,4,32,256]{4,3,2,1,0:T(8,128)S(1)}, u32[]{:S(2)}, u32[]{:S(2)}) collective-permute-start(f32[2,2,4,32,256]{4,3,2,1,0:T(8,128)S(1)} %shard_map.138), channel_id=1, source_target_pairs={{0,4},{1,5},{2,6},{3,7},{4,0},{5,1},{6,2},{7,3},{8,12},{9,13},{10,... | collective-permute-start | bytes 1572872 | tf_op jit(solution)/shard_map/ppermute | solution.py:490
  4.8 1.6 %shard_map.137 = (f32[2,16,8,256]{3,2,1,0:T(8,128)S(1)}, f32[2,16,8,256]{3,2,1,0:T(8,128)S(1)}) custom-call(f32[2,16,32,256]{3,2,1,0:T(8,128)} %u_old.3, f32[2,16,32,256]{3,2,1,0:T(8,128)} %a_old.3, f32[16,32,256]{2,1,0:T(8,128)} %cour.11), custom_call_target="tpu_custom_call" | custom-call | flops 1048576 | bytes 1048576 | tf_op jit(solution)/shard_map/pallas_call | solution.py:462
  6.4 0.0 copy-start.8
  6.4 0.0 copy-start.7
  6.4 2.6 %collective-permute-start = (f32[2,16,8,256]{3,2,1,0:T(8,128)S(1)}, f32[2,16,8,256]{3,2,1,0:T(8,128)S(1)}, u32[]{:S(2)}, u32[]{:S(2)}) collective-permute-start(f32[2,16,8,256]{3,2,1,0:T(8,128)S(1)} %get-tuple-element.32), channel_id=1, source_target_pairs={{0,1},{4,5},{2,3},{6,7},{1,0},{5,4},{3,2},{7,6},{8,9},{12,13},{10,... | collective-permute-start | bytes 786440 | tf_op jit(solution)/shard_map/ppermute | solution.py:490
  9.0 0.1 collective-permute-start.1
  9.2 2.5 %shard_map.139 = (f32[2,16,32,256]{3,2,1,0:T(8,128)S(1)}, f32[2,16,32,128]{3,2,1,0:T(8,128)S(1)}, bf16[32,96]{1,0:T(8,128)(2,1)S(1)}, bf16[768,256]{1,0:T(8,128)(2,1)S(1)}) custom-call(s32[2]{0:T(128)S(1)} %copy-done.6, s32[2]{0:T(128)S(1)} %copy-done.8, f32[2,128]{1,0:T(2,128)S(1)} %copy-done.7, f32[2,16,32,256]{3,2,1,0:T(8,128)S(1)} %copy-done.5, ...), custom_call_target="tpu_custom_call" | custom-call | flops 8388608 | bytes 8388608 | tf_op jit(solution)/shard_map/pallas_call | solution.py:462
  11.6 3.0 %shard_map.140.refs_5_.refs_4_ = f32[2,16,32,256]{3,2,1,0:T(8,128)S(1)} custom-call(s32[2]{0:T(128)S(1)} %copy-done.6, s32[2,1024]{1,0:T(2,128)} %rec_hbm.3, f32[2,128,1024]{2,1,0:T(8,128)} %trace_hbm.3, f32[2,16,32,256]{3,2,1,0:T(8,128)S(1)} %copy-done.3, f32[2,16,32,256]{3,2,1,0:T(8,128)} %a_old.2, f32[16,32,256]{2,1,0:T(8,128)S(1)} %copy-done.1, ...), custom_call_target="tpu_custom_call" | custom-call | flops 8388608 | bytes 8388608 | tf_op jit(solution)/shard_map/pallas_call | solution.py:462
  14.6 1.2 %collective-permute-done.refs_0_ = f32[2,16,8,256]{3,2,1,0:T(8,128)S(1)} collective-permute-done((f32[2,16,8,256]{3,2,1,0:T(8,128)S(1)}, f32[2,16,8,256]{3,2,1,0:T(8,128)S(1)}, u32[]{:S(2)}, u32[]{:S(2)}) %collective-permute-start) | collective-permute-done | bytes 262176 | tf_op jit(solution)/shard_map/ppermute | solution.py:490
  15.9 0.5 %shard_map.141 = (f32[2,16,32,256]{3,2,1,0:T(8,128)S(1)}, f32[2,16,32,128]{3,2,1,0:T(8,128)S(1)}, f32[1,16,8,256]{3,2,1,0:T(8,128)S(1)}, f32[1,16,8,256]{3,2,1,0:T(8,128)S(1)}, f32[1,2,4,32,256]{4,3,2,1,0:T(8,128)S(1)}) custom-call(f32[2,16,8,256]{3,2,1,0:T(8,128)S(1)} %collective-permute-done.refs_0_, ...), custom_call_target="tpu_custom_call", output_to_operand_aliasing={{0}: (6, {}), {1}: (7, {})} | custom-call | flops 1048576 | bytes 1048576 | tf_op jit(solution)/shard_map/pallas_call | solution.py:462
  16.3 0.1 collective-permute-start.5
  16.4 2.9 %collective-permute-start.3 = (f32[1,16,8,256]{3,2,1,0:T(8,128)S(1)}, f32[1,16,8,256]{3,2,1,0:T(8,128)S(1)}, u32[]{:S(2)}, u32[]{:S(2)}) collective-permute-start(f32[1,16,8,256]{3,2,1,0:T(8,128)S(1)} %get-tuple-element.42), channel_id=1, source_target_pairs={{0,1},{4,5},{2,3},{6,7},{1,0},{5,4},{3,2},{7,6},{8,9},{12,13},{10,... | collective-permute-start | bytes 393224 | tf_op jit(solution)/shard_map/ppermute | solution.py:490
  19.4 0.2 collective-permute-start.4
  19.5 0.4 %shard_map.142 = (f32[2,16,32,256]{3,2,1,0:T(8,128)S(1)}, f32[1,16,8,256]{3,2,1,0:T(8,128)S(1)}, f32[1,16,8,256]{3,2,1,0:T(8,128)S(1)}, f32[1,2,4,32,256]{4,3,2,1,0:T(8,128)S(1)}) custom-call(f32[2,16,8,256]{3,2,1,0:T(8,128)S(1)} %collective-permute-done.refs_0_, ...), custom_call_target="tpu_custom_call", output_to_operand_aliasing={{0}: (4, {})} | custom-call | flops 1048576 | bytes 1048576 | tf_op jit(solution)/shard_map/pallas_call | solution.py:462
  19.9 0.4 %collective-permute-start.8 = (f32[1,2,4,32,256]{4,3,2,1,0:T(8,128)S(1)}, f32[1,2,4,32,256]{4,3,2,1,0:T(8,128)S(1)}, u32[]{:S(2)}, u32[]{:S(2)}) collective-permute-start(f32[1,2,4,32,256]{4,3,2,1,0:T(8,128)S(1)} %get-tuple-element.52), channel_id=1, source_target_pairs={{0,4},{1,5},{2,6},{3,7},{4,0},{5,1},{6,2},{7,3},{8,12},{9,13},{10,... | collective-permute-start | bytes 786440 | tf_op jit(solution)/shard_map/ppermute | solution.py:490
  20.3 1.6 %collective-permute-start.6 = (f32[1,16,8,256]{3,2,1,0:T(8,128)S(1)}, f32[1,16,8,256]{3,2,1,0:T(8,128)S(1)}, u32[]{:S(2)}, u32[]{:S(2)}) collective-permute-start(f32[1,16,8,256]{3,2,1,0:T(8,128)S(1)} %get-tuple-element.50), channel_id=1, source_target_pairs={{0,1},{4,5},{2,3},{6,7},{1,0},{5,4},{3,2},{7,6},{8,9},{12,13},{10,... | collective-permute-start | bytes 393224 | tf_op jit(solution)/shard_map/ppermute | solution.py:490
  21.9 2.3 %shard_map.143 = (f32[2,16,32,256]{3,2,1,0:T(8,128)S(1)}, f32[2,16,32,128]{3,2,1,0:T(8,128)S(1)}, f32[2,16,32,256]{3,2,1,0:T(8,128)}) custom-call(s32[2]{0:T(128)S(1)} %copy-done.6, s32[2]{0:T(128)S(1)} %copy-done.8, f32[2,128]{1,0:T(2,128)S(1)} %copy-done.7, f32[2,16,32,256]{3,2,1,0:T(8,128)S(1)} %get-tuple-element.38.u, f32[2,16,32,256]{3,2,1,0:T(8,128)S(1)} %copy-done.5, ...), custom_call_target="tpu_custom_call" | custom-call | flops 8388608 | bytes 8388608 | tf_op jit(solution)/shard_map/pallas_call | solution.py:462
  24.3 0.2 collective-permute-start.7
  24.5 0.8 %shard_map.144 = (f32[2,16,32,256]{3,2,1,0:T(8,128)S(1)}, f32[2,16,32,128]{3,2,1,0:T(8,128)S(1)}, f32[16,16,128]{2,1,0:T(8,128)S(1)}, f32[16,16,128]{2,1,0:T(8,1...) custom-call(f32[1,16,8,256]{3,2,1,0:T(8,128)S(1)} %collective-permut, ...), custom_call_target="tpu_custom_call", output_to_operand_aliasing={{0}: (5, {}), {1}: (6, {})} | custom-call | flops 1048576 | bytes 1048576 | tf_op jit(solution)/shard_map/pallas_call | solution.py:462
  25.3 2.5 %collective-permute-start.9 = (f32[16,16,128]{2,1,0:T(8,128)S(1)}, f32[16,16,128]{2,1,0:T(8,128)S(1)}, u32[]{:S(2)}, u32[]{:S(2)}) collective-permute-start(f32[16,16,128]{2,1,0:T(8,128)S(1)} %get-tuple-element.56), channel_id=1, source_target_pairs={{0,24},{8,16},{16,8},{24,0},{1,25},{9,17},{17,9},{25,1},{2,26},{10... | collective-permute-start | bytes 393224 | tf_op jit(solution)/shard_map/ppermute | solution.py:577
  27.9 0.5 %collective-permute-start.10 = (f32[16,16,128]{2,1,0:T(8,128)S(1)}, f32[16,16,128]{2,1,0:T(8,128)S(1)}, u32[]{:S(2)}, u32[]{:S(2)}) collective-permute-start(f32[16,16,128]{2,1,0:T(8,128)S(1)} %get-tuple-element.57), channel_id=1, source_target_pairs={{0,8},{8,0},{16,24},{24,16},{1,9},{9,1},{17,25},{25,17},{2,10},{10... | collective-permute-start | bytes 393224 | tf_op jit(solution)/shard_map/ppermute | solution.py:577
  28.4 0.5 %collective-permute-start.11 = (f32[16,16,128]{2,1,0:T(8,128)S(1)}, f32[16,16,128]{2,1,0:T(8,128)S(1)}, u32[]{:S(2)}, u32[]{:S(2)}) collective-permute-start(f32[16,16,128]{2,1,0:T(8,128)S(1)} %get-tuple-element.58), channel_id=1, source_target_pairs={{0,16},{8,24},{16,0},{24,8},{1,17},{9,25},{17,1},{25,9},{2,18},{10... | collective-permute-start | bytes 393224 | tf_op jit(solution)/shard_map/ppermute | solution.py:577
  28.9 2.8 %shard_map.145 = (f32[2,16,32,256]{3,2,1,0:T(8,128)S(1)}, f32[2,16,32,256]{3,2,1,0:T(8,128)}, f32[2,16,32,256]{3,2,1,0:T(8,128)}) custom-call(s32[2]{0:T(128)S(1)} %copy-done.6, s32[2,1024]{1,0:T(2,128)} %rec_hbm.3, f32[2,128,1024]{2,1,0:T(8,128)} %trace_hbm.3, f32[2,16,32,256]{3,2,1,0:T(8,128)S(1)} %get-tuple-element.39.a.refs_3_, ...), custom_call_target="tpu_custom_call" | custom-call | flops 8388608 | bytes 8388608 | tf_op jit(solution)/shard_map/pallas_call | solution.py:462
  31.7 1.3 %shard_map.146 = (f32[2,16,32,256]{3,2,1,0:T(8,128)S(1)}, f32[2,16,32,256]{3,2,1,0:T(8,128)}) custom-call(f32[1,16,8,256]{3,2,1,0:T(8,128)S(1)} %collective-permute-done.6.refs_0_, f32[1,16,8,256]{3,2,1,0:T(8,128)S(1)} %collective-permute-done.7.refs_1_, f32[1,2,4,32,256]{4,3,2,1,0:T(8,128)S(1)} %collective-permute-done.8.refs_2_, ...), custom_call_target="tpu_custom_call", output_to_operand_aliasing={{0}: (4, {})} | custom-call | flops 1048576 | bytes 1048576 | tf_op jit(solution)/shard_map/pallas_call | solution.py:462
  33.0 2.0 %collective-permute-done.10.second = f32[16,16,128]{2,1,0:T(8,128)S(1)} collective-permute-done((f32[16,16,128]{2,1,0:T(8,128)S(1)}, f32[16,16,128]{2,1,0:T(8,128)S(1)}, u32[]{:S(2)}, u32[]{:S(2)}) %collective-permute-start.10) | collective-permute-done | bytes 131104 | tf_op jit(solution)/shard_map/ppermute | solution.py:577
  35.0 1.4 %shard_map.147 = f32[16,32,64]{2,1,0:T(8,128)} custom-call(f32[16,32,256]{2,1,0:T(8,128)S(1)} %copy-done.1, f32[16,16,128]{2,1,0:T(8,128)S(1)} %get-tuple-element.55.own, f32[16,16,128]{2,1,0:T(8,128)S(1)} %collective-permute-done.9.first, f32[16,16,128]{2,1,0:T(8,128)S(1)} %collective-permute-done.10.second, f32[16,16,128]{2,1,0:T(8,128)S(1)} %collective-permute-done.11.third), custom_call_target="tpu_custom_call" | custom-call | flops 1048576 | bytes 1048576 | tf_op jit(solution)/shard_map/pallas_call | solution.py:462
  (21 shorter events, 0.1 us)
Async XLA Ops:
  0.6 1.0 %copy-start = (f32[16,32,256]{2,1,0:T(8,128)S(1)}, f32[16,32,256]{2,1,0:T(8,128)}, u32[]{:S(2)}) copy-start(f32[16,32,256]{2,1,0:T(8,128)} %cour.11) | copy-start | bytes 1572868
  1.7 1.2 %copy-start.2 = (f32[2,16,32,256]{3,2,1,0:T(8,128)S(1)}, f32[2,16,32,256]{3,2,1,0:T(8,128)}, u32[]{:S(2)}) copy-start(f32[2,16,32,256]{3,2,1,0:T(8,128)} %a_old.3) | copy-start | bytes 3145732
  2.9 1.2 %copy-start.4 = (f32[2,16,32,256]{3,2,1,0:T(8,128)S(1)}, f32[2,16,32,256]{3,2,1,0:T(8,128)}, u32[]{:S(2)}) copy-start(f32[2,16,32,256]{3,2,1,0:T(8,128)} %u_old.3) | copy-start | bytes 3145732
  4.2 5.0 %copy-start.1 = (f32[16,32,256]{2,1,0:T(8,128)S(1)}, f32[16,32,256]{2,1,0:T(8,128)}, u32[]{:S(2)}) copy-start(f32[16,32,256]{2,1,0:T(8,128)} %cour.11) | copy-start | bytes 1572868
  4.2 4.9 %copy-start.3 = (f32[2,16,32,256]{3,2,1,0:T(8,128)S(1)}, f32[2,16,32,256]{3,2,1,0:T(8,128)}, u32[]{:S(2)}) copy-start(f32[2,16,32,256]{3,2,1,0:T(8,128)} %a_old.3) | copy-start | bytes 3145732
  4.2 4.9 %copy-start.5 = (f32[2,16,32,256]{3,2,1,0:T(8,128)S(1)}, f32[2,16,32,256]{3,2,1,0:T(8,128)}, u32[]{:S(2)}) copy-start(f32[2,16,32,256]{3,2,1,0:T(8,128)} %u_old.3) | copy-start | bytes 3145732
  4.2 11.7 %collective-permute-start.2 = (f32[2,2,4,32,256]{4,3,2,1,0:T(8,128)S(1)}, f32[2,2,4,32,256]{4,3,2,1,0:T(8,128)S(1)}, u32[]{:S(2)}, u32[]{:S(2)}) collective-permute-start(f32[2,2,4,32,256]{4,3,2,1,0:T(8,128)S(1)} %shard_map.138), channel_id=1, source_target_pairs={{0,4},{1,5},{2,6},{3,7},{4,0},{5,1},{6,2},{7,3},{8,12},{9,13},{10,... | collective-permute-start | bytes 1572872 | tf_op jit(solution)/shard_map/ppermute | solution.py:490
  6.4 2.7 %copy-start.8 = (s32[2]{0:T(128)S(1)}, s32[2]{0:T(128)}, u32[]{:S(2)}) copy-start(s32[2]{0:T(128)} %src_ref.3) | copy-start | bytes 28
  6.4 2.7 %copy-start.6 = (s32[2]{0:T(128)S(1)}, s32[2]{0:T(128)}, u32[]{:S(2)}) copy-start(s32[2]{0:T(128)} %step_ref.7) | copy-start | bytes 28
  6.4 2.7 %copy-start.7 = (f32[2,128]{1,0:T(2,128)S(1)}, f32[2,128]{1,0:T(2,128)}, u32[]{:S(2)}) copy-start(f32[2,128]{1,0:T(2,128)} %wave_ref.3) | copy-start | bytes 3076
  6.4 9.4 %collective-permute-start = (f32[2,16,8,256]{3,2,1,0:T(8,128)S(1)}, f32[2,16,8,256]{3,2,1,0:T(8,128)S(1)}, u32[]{:S(2)}, u32[]{:S(2)}) collective-permute-start(f32[2,16,8,256]{3,2,1,0:T(8,128)S(1)} %get-tuple-element.32), channel_id=1, source_target_pairs={{0,1},{4,5},{2,3},{6,7},{1,0},{5,4},{3,2},{7,6},{8,9},{12,13},{10,... | collective-permute-start | bytes 786440 | tf_op jit(solution)/shard_map/ppermute | solution.py:490
  9.0 6.8 %collective-permute-start.1 = (f32[2,16,8,256]{3,2,1,0:T(8,128)S(1)}, f32[2,16,8,256]{3,2,1,0:T(8,128)S(1)}, u32[]{:S(2)}, u32[]{:S(2)}) collective-permute-start(f32[2,16,8,256]{3,2,1,0:T(8,128)S(1)} %get-tuple-element.33), channel_id=1, source_target_pairs={{1,2},{5,6},{2,1},{6,5},{0,4},{4,0},{3,7},{7,3},{9,10},{13,14},{10... | collective-permute-start | bytes 786440 | tf_op jit(solution)/shard_map/ppermute | solution.py:490
  16.3 8.2 %collective-permute-start.5 = (f32[1,2,4,32,256]{4,3,2,1,0:T(8,128)S(1)}, f32[1,2,4,32,256]{4,3,2,1,0:T(8,128)S(1)}, u32[]{:S(2)}, u32[]{:S(2)}) collective-permute-start(f32[1,2,4,32,256]{4,3,2,1,0:T(8,128)S(1)} %get-tuple-element.44), channel_id=1, source_target_pairs={{0,4},{1,5},{2,6},{3,7},{4,0},{5,1},{6,2},{7,3},{8,12},{9,13},{10,... | collective-permute-start | bytes 786440 | tf_op jit(solution)/shard_map/ppermute | solution.py:490
  16.4 7.9 %collective-permute-start.3 = (f32[1,16,8,256]{3,2,1,0:T(8,128)S(1)}, f32[1,16,8,256]{3,2,1,0:T(8,128)S(1)}, u32[]{:S(2)}, u32[]{:S(2)}) collective-permute-start(f32[1,16,8,256]{3,2,1,0:T(8,128)S(1)} %get-tuple-element.42), channel_id=1, source_target_pairs={{0,1},{4,5},{2,3},{6,7},{1,0},{5,4},{3,2},{7,6},{8,9},{12,13},{10,... | collective-permute-start | bytes 393224 | tf_op jit(solution)/shard_map/ppermute | solution.py:490
  19.4 5.2 %collective-permute-start.4 = (f32[1,16,8,256]{3,2,1,0:T(8,128)S(1)}, f32[1,16,8,256]{3,2,1,0:T(8,128)S(1)}, u32[]{:S(2)}, u32[]{:S(2)}) collective-permute-start(f32[1,16,8,256]{3,2,1,0:T(8,128)S(1)} %get-tuple-element.43), channel_id=1, source_target_pairs={{1,2},{5,6},{2,1},{6,5},{0,4},{4,0},{3,7},{7,3},{9,10},{13,14},{10... | collective-permute-start | bytes 393224 | tf_op jit(solution)/shard_map/ppermute | solution.py:490
  19.9 11.8 %collective-permute-start.8 = (f32[1,2,4,32,256]{4,3,2,1,0:T(8,128)S(1)}, f32[1,2,4,32,256]{4,3,2,1,0:T(8,128)S(1)}, u32[]{:S(2)}, u32[]{:S(2)}) collective-permute-start(f32[1,2,4,32,256]{4,3,2,1,0:T(8,128)S(1)} %get-tuple-element.52), channel_id=1, source_target_pairs={{0,4},{1,5},{2,6},{3,7},{4,0},{5,1},{6,2},{7,3},{8,12},{9,13},{10,... | collective-permute-start | bytes 786440 | tf_op jit(solution)/shard_map/ppermute | solution.py:490
  20.3 8.0 %collective-permute-start.6 = (f32[1,16,8,256]{3,2,1,0:T(8,128)S(1)}, f32[1,16,8,256]{3,2,1,0:T(8,128)S(1)}, u32[]{:S(2)}, u32[]{:S(2)}) collective-permute-start(f32[1,16,8,256]{3,2,1,0:T(8,128)S(1)} %get-tuple-element.50), channel_id=1, source_target_pairs={{0,1},{4,5},{2,3},{6,7},{1,0},{5,4},{3,2},{7,6},{8,9},{12,13},{10,... | collective-permute-start | bytes 393224 | tf_op jit(solution)/shard_map/ppermute | solution.py:490
  24.3 7.4 %collective-permute-start.7 = (f32[1,16,8,256]{3,2,1,0:T(8,128)S(1)}, f32[1,16,8,256]{3,2,1,0:T(8,128)S(1)}, u32[]{:S(2)}, u32[]{:S(2)}) collective-permute-start(f32[1,16,8,256]{3,2,1,0:T(8,128)S(1)} %get-tuple-element.51), channel_id=1, source_target_pairs={{1,2},{5,6},{2,1},{6,5},{0,4},{4,0},{3,7},{7,3},{9,10},{13,14},{10... | collective-permute-start | bytes 393224 | tf_op jit(solution)/shard_map/ppermute | solution.py:490
  25.3 7.7 %collective-permute-start.9 = (f32[16,16,128]{2,1,0:T(8,128)S(1)}, f32[16,16,128]{2,1,0:T(8,128)S(1)}, u32[]{:S(2)}, u32[]{:S(2)}) collective-permute-start(f32[16,16,128]{2,1,0:T(8,128)S(1)} %get-tuple-element.56), channel_id=1, source_target_pairs={{0,24},{8,16},{16,8},{24,0},{1,25},{9,17},{17,9},{25,1},{2,26},{10... | collective-permute-start | bytes 393224 | tf_op jit(solution)/shard_map/ppermute | solution.py:577
  27.9 7.1 %collective-permute-start.10 = (f32[16,16,128]{2,1,0:T(8,128)S(1)}, f32[16,16,128]{2,1,0:T(8,128)S(1)}, u32[]{:S(2)}, u32[]{:S(2)}) collective-permute-start(f32[16,16,128]{2,1,0:T(8,128)S(1)} %get-tuple-element.57), channel_id=1, source_target_pairs={{0,8},{8,0},{16,24},{24,16},{1,9},{9,1},{17,25},{25,17},{2,10},{10... | collective-permute-start | bytes 393224 | tf_op jit(solution)/shard_map/ppermute | solution.py:577
  28.4 6.6 %collective-permute-start.11 = (f32[16,16,128]{2,1,0:T(8,128)S(1)}, f32[16,16,128]{2,1,0:T(8,128)S(1)}, u32[]{:S(2)}, u32[]{:S(2)}) collective-permute-start(f32[16,16,128]{2,1,0:T(8,128)S(1)} %get-tuple-element.58), channel_id=1, source_target_pairs={{0,16},{8,24},{16,0},{24,8},{1,17},{9,25},{17,1},{25,9},{2,18},{10... | collective-permute-start | bytes 393224 | tf_op jit(solution)/shard_map/ppermute | solution.py:577
where the time goes:
time: 36.6 us; the launch traced here: 36.3 us
  Pallas kernels  16.6 us (45%)
  starting transfers between devices  12.2 us (33%)
  local copies, waits for them, and re-layouts  3.52 us (10%)
  waiting for transfers between devices  3.22 us (9%)
  between operations  0.83 us (2%)
    pallas_call x11, Pallas kernels, call(): pl.pallas_call(body, out_shape=outs, in_specs=in_specs, out_specs=out_spe...  16.6 us
    ppermute x9, starting transfers between devices, swap(): halos.append(lax.ppermute(send, ('gx', 'gy'), perm))  8.63 us
    ppermute x3, starting transfers between devices, shards(): lax.ppermute(u_sends[k], 'shot', [(i, i ^ k) for i in range(groups)])  3.55 us
    unnamed x18, local copies, waits for them, and re-layouts  3.52 us
    ppermute x3, waiting for transfers between devices, shards(): lax.ppermute(u_sends[k], 'shot', [(i, i ^ k) for i in range(groups)])  1.96 us
    ppermute x9, waiting for transfers between devices, swap(): halos.append(lax.ppermute(send, ('gx', 'gy'), perm))  1.26 us
  transfers between devices with their start and end apart: 12, of which 2 were waited for; matrix products, arithmetic and copies ran while one was open for 0% of the time, Pallas kernels for 40%

commit v1 on v0

--- a/solution.py
+++ b/solution.py
@@ -92,6 +92,7 @@
 
 def first_y_sends(u_hbm, a_hbm, c_hbm, *refs):
     *ys, u_low, u_high, a_low, a_high, c_low, c_high, sems = refs
+    forward, adjoint = ys[: len(ys) // 2], ys[len(ys) // 2 :]
     _, width_x, width_y, depth = u_hbm.shape
     copies = Copies(sems)
     waits = []
@@ -107,10 +108,10 @@
         for z in halves(depth):
             low = c_low[x, :, z] * c_low[x, :, z]
             high = c_high[x, :, z] * c_high[x, :, z]
-            write_y_sends(ys, 0, x, z, *(ref[s, x, :, z] for ref in (u_low, u_high) for s in range(2)))
+            write_y_sends(forward, 0, x, z, *(ref[s, x, :, z] for ref in (u_low, u_high) for s in range(2)))
             write_y_sends(
-                ys,
-                1,
+                adjoint,
+                0,
                 x,
                 z,
                 *(m * ref[s, x, :, z] for m, ref in ((low, a_low), (high, a_high)) for s in range(2)),
@@ -155,7 +156,7 @@
     return top, middle, (rest - middle.astype(F32)).astype(BF16)
 
 
-BATCH = 8
+BATCH = 16
 
 
 def plane_stencil(block_of, shots, band_y, band_z, split, flat):
@@ -339,8 +340,8 @@
 
     def rows(x, carry):
         for h, z in enumerate(halves(depth)):
-            first = hy[0][field_at, x, :, z]
-            second = hy[1][field_at, x, :, z] if len(hy) > 1 else jnp.zeros_like(first)
+            first = hy[0][0, x, :, z]
+            second = hy[1][0, x, :, z] if len(hy) > 1 else jnp.zeros_like(first)
             below = jnp.where(has_below, jnp.where(even, second, first), 0.0)
             above = jnp.where(has_above, jnp.where(even, first, second), 0.0)
             for side in range(2):
@@ -496,13 +497,14 @@
     y_rows = (shots, width_x, 8, depth)
     first_y = call(
         first_y_sends,
-        [shape(2, *y_send)] * turns_y,
+        [shape(1, *y_send)] * (2 * turns_y),
         [pltpu.VMEM(y_rows, F32)] * 4 + [pltpu.VMEM(y_rows[1:], F32)] * 2 + [pltpu.SemaphoreType.DMA((6,))],
         [HBM] * 3,
         (in_hbm(fwd_now), in_hbm(adj_now), in_hbm(courant)),
         1 << 20,
     )
-    hy_u = hy_a = swap(first_y, perms_y)
+    hy_u = swap(first_y[:turns_y], perms_y)
+    hy_a = swap(first_y[turns_y:], perms_y)
     first_x = call(
         first_x_sends,
         [shape(2, *x_rows)] * turns_x,

time: 36.6 us -> 40.5 us (1.11)
  starting transfers between devices: 12.2 us -> 15.8 us
  Pallas kernels: 16.6 us -> 17.1 us
    ppermute x9 -> x11, starting transfers between devices: 8.63 us -> 12.2 us  [swap(): halos.append(lax.ppermute(send, ('gx', 'gy'), perm))]
    pallas_call x11, Pallas kernels: 16.6 us -> 17.1 us  [call(): pl.pallas_call(body, out_shape=outs, in_specs=in_specs, out_specs=out_spe...]
    ppermute x9 -> x11, waiting for transfers between devices: 1.26 us -> 0.97 us  [swap(): halos.append(lax.ppermute(send, ('gx', 'gy'), perm))]
  transfers between devices with their start and end apart: 12 -> 14, of which waited for: 2 -> 2; matrix products, arithmetic and copies ran while one was open for 0% -> 0% of each run, Pallas kernels for 40% -> 39%
where the time goes in v1:
time: 40.5 us; the launch traced here: 40.2 us
  Pallas kernels  17.1 us (42%)
  starting transfers between devices  15.8 us (39%)
  local copies, waits for them, and re-layouts  3.52 us (9%)
  waiting for transfers between devices  3.03 us (7%)
  between operations  0.83 us (2%)
    pallas_call x11, Pallas kernels, call(): pl.pallas_call(body, out_shape=outs, in_specs=in_specs, out_specs=out_spe...  17.1 us
    ppermute x11, starting transfers between devices, swap(): halos.append(lax.ppermute(send, ('gx', 'gy'), perm))  12.2 us
    ppermute x3, starting transfers between devices, shards(): lax.ppermute(u_sends[k], 'shot', [(i, i ^ k) for i in range(groups)])  3.55 us
    unnamed x18, local copies, waits for them, and re-layouts  3.52 us
    ppermute x3, waiting for transfers between devices, shards(): lax.ppermute(u_sends[k], 'shot', [(i, i ^ k) for i in range(groups)])  2.06 us
    ppermute x11, waiting for transfers between devices, swap(): halos.append(lax.ppermute(send, ('gx', 'gy'), perm))  0.97 us
  transfers between devices with their start and end apart: 14, of which 2 were waited for; matrix products, arithmetic and copies ran while one was open for 0% of the time, Pallas kernels for 39%

profile of v1, /device:TPU:0, one launch (start us, length us, event | category | flops | bytes accessed | tf_op | source)
XLA Modules:
  0.0 40.2 jit_solution(8819997206278436499)
XLA Ops:
  0.6 0.0 copy-start
  0.6 1.0 %copy-done = f32[16,32,256]{2,1,0:T(8,128)S(1)} copy-done((f32[16,32,256]{2,1,0:T(8,128)S(1)}, f32[16,32,256]{2,1,0:T(8,128)}, u32[]{:S(2)}) %copy-start) | copy-done | bytes 524312
  1.7 1.2 %copy-done.2 = f32[2,16,32,256]{3,2,1,0:T(8,128)S(1)} copy-done((f32[2,16,32,256]{3,2,1,0:T(8,128)S(1)}, f32[2,16,32,256]{3,2,1,0:T(8,128)}, u32[]{:S(2)}) %copy-start.2) | copy-done | bytes 1048600
  2.9 1.2 %copy-done.4 = f32[2,16,32,256]{3,2,1,0:T(8,128)S(1)} copy-done((f32[2,16,32,256]{3,2,1,0:T(8,128)S(1)}, f32[2,16,32,256]{3,2,1,0:T(8,128)}, u32[]{:S(2)}) %copy-start.4) | copy-done | bytes 1048600
  4.2 0.0 copy-start.1
  4.2 0.0 copy-start.3
  4.2 0.0 copy-start.5
  4.2 0.6 %collective-permute-start.2 = (f32[2,2,4,32,256]{4,3,2,1,0:T(8,128)S(1)}, f32[2,2,4,32,256]{4,3,2,1,0:T(8,128)S(1)}, u32[]{:S(2)}, u32[]{:S(2)}) collective-permute-start(f32[2,2,4,32,256]{4,3,2,1,0:T(8,128)S(1)} %shard_map.138), channel_id=1, source_target_pairs={{0,4},{1,5},{2,6},{3,7},{4,0},{5,1},{6,2},{7,3},{8,12},{9,13},{10,... | collective-permute-start | bytes 1572872 | tf_op jit(solution)/shard_map/ppermute | solution.py:491
  4.8 1.6 %shard_map.137 = (f32[1,16,8,256]{3,2,1,0:T(8,128)S(1)}, f32[1,16,8,256]{3,2,1,0:T(8,128)S(1)}, f32[1,16,8,256]{3,2,1,0:T(8,128)S(1)}, f32[1,16,8,256]{3,2,1,0:T(8,128)S(1)}) custom-call(f32[2,16,32,256]{3,2,1,0:T(8,128)} %u_old.3, f32[2,16,32,256]{3,2,1,0:T(8,128)} %a_old.3, f32[16,32,256]{2,1,0:T(8,128)} %cour.11), custom_call_target="tpu_custom_call" | custom-call | flops 1048576 | bytes 1048576 | tf_op jit(solution)/shard_map/pallas_call | solution.py:463
  6.4 2.6 %collective-permute-start = (f32[1,16,8,256]{3,2,1,0:T(8,128)S(1)}, f32[1,16,8,256]{3,2,1,0:T(8,128)S(1)}, u32[]{:S(2)}, u32[]{:S(2)}) collective-permute-start(f32[1,16,8,256]{3,2,1,0:T(8,128)S(1)} %get-tuple-element.34), channel_id=1, source_target_pairs={{0,1},{4,5},{2,3},{6,7},{1,0},{5,4},{3,2},{7,6},{8,9},{12,13},{10,... | collective-permute-start | bytes 393224 | tf_op jit(solution)/shard_map/ppermute | solution.py:491
  9.0 0.1 collective-permute-start.1
  9.1 3.1 %collective-permute-start.3 = (f32[1,16,8,256]{3,2,1,0:T(8,128)S(1)}, f32[1,16,8,256]{3,2,1,0:T(8,128)S(1)}, u32[]{:S(2)}, u32[]{:S(2)}) collective-permute-start(f32[1,16,8,256]{3,2,1,0:T(8,128)S(1)} %get-tuple-element.41), channel_id=1, source_target_pairs={{0,1},{4,5},{2,3},{6,7},{1,0},{5,4},{3,2},{7,6},{8,9},{12,13},{10,... | collective-permute-start | bytes 393224 | tf_op jit(solution)/shard_map/ppermute | solution.py:491
  12.2 2.8 %shard_map.139 = (f32[2,16,32,256]{3,2,1,0:T(8,128)S(1)}, f32[2,16,32,128]{3,2,1,0:T(8,128)S(1)}, bf16[32,96]{1,0:T(8,128)(2,1)S(1)}, bf16[768,256]{1,0:T(8,128)(2,1)S(1)}) custom-call(s32[2]{0:T(128)S(1)} %copy-done.6, s32[2]{0:T(128)S(1)} %copy-done.8, f32[2,128]{1,0:T(2,128)S(1)} %copy-done.7, f32[2,16,32,256]{3,2,1,0:T(8,128)S(1)} %copy-done.5, ...), custom_call_target="tpu_custom_call" | custom-call | flops 8388608 | bytes 8388608 | tf_op jit(solution)/shard_map/pallas_call | solution.py:463
  15.0 3.4 %shard_map.140.refs_5_.refs_4_ = f32[2,16,32,256]{3,2,1,0:T(8,128)S(1)} custom-call(s32[2]{0:T(128)S(1)} %copy-done.6, s32[2,1024]{1,0:T(2,128)} %rec_hbm.3, f32[2,128,1024]{2,1,0:T(8,128)} %trace_hbm.3, f32[2,16,32,256]{3,2,1,0:T(8,128)S(1)} %copy-done.3, f32[2,16,32,256]{3,2,1,0:T(8,128)} %a_old.2, f32[16,32,256]{2,1,0:T(8,128)S(1)} %copy-done.1, ...), custom_call_target="tpu_custom_call" | custom-call | flops 8388608 | bytes 8388608 | tf_op jit(solution)/shard_map/pallas_call | solution.py:463
  18.5 0.5 %shard_map.141 = (f32[2,16,32,256]{3,2,1,0:T(8,128)S(1)}, f32[2,16,32,128]{3,2,1,0:T(8,128)S(1)}, f32[1,16,8,256]{3,2,1,0:T(8,128)S(1)}, f32[1,16,8,256]{3,2,1,0:T(8,128)S(1)}, f32[1,2,4,32,256]{4,3,2,1,0:T(8,128)S(1)}) custom-call(f32[1,16,8,256]{3,2,1,0:T(8,128)S(1)} %collective-permute-done.refs_0_, ...), custom_call_target="tpu_custom_call", output_to_operand_aliasing={{0}: (6, {}), {1}: (7, {})} | custom-call | flops 1048576 | bytes 1048576 | tf_op jit(solution)/shard_map/pallas_call | solution.py:463
  19.0 0.1 collective-permute-start.7
  19.0 0.5 %collective-permute-start.4 = (f32[1,16,8,256]{3,2,1,0:T(8,128)S(1)}, f32[1,16,8,256]{3,2,1,0:T(8,128)S(1)}, u32[]{:S(2)}, u32[]{:S(2)}) collective-permute-start(f32[1,16,8,256]{3,2,1,0:T(8,128)S(1)} %get-tuple-element.42), channel_id=1, source_target_pairs={{1,2},{5,6},{2,1},{6,5},{0,4},{4,0},{3,7},{7,3},{9,10},{13,14},{10... | collective-permute-start | bytes 393224 | tf_op jit(solution)/shard_map/ppermute | solution.py:491
  19.5 0.3 collective-permute-start.5
  19.8 0.9 %collective-permute-done.4.refs_1_ = f32[1,16,8,256]{3,2,1,0:T(8,128)S(1)} collective-permute-done((f32[1,16,8,256]{3,2,1,0:T(8,128)S(1)}, f32[1,16,8,256]{3,2,1,0:T(8,128)S(1)}, u32[]{:S(2)}, u32[]{:S(2)}) %collective-permute-start.4) | collective-permute-done | bytes 131104 | tf_op jit(solution)/shard_map/ppermute | solution.py:491
  20.7 0.4 %shard_map.142 = (f32[2,16,32,256]{3,2,1,0:T(8,128)S(1)}, f32[1,16,8,256]{3,2,1,0:T(8,128)S(1)}, f32[1,16,8,256]{3,2,1,0:T(8,128)S(1)}, f32[1,2,4,32,256]{4,3,2,1,0:T(8,128)S(1)}) custom-call(f32[1,16,8,256]{3,2,1,0:T(8,128)S(1)} %collective-permute-done.3.refs_0_, ...), custom_call_target="tpu_custom_call", output_to_operand_aliasing={{0}: (4, {})} | custom-call | flops 1048576 | bytes 1048576 | tf_op jit(solution)/shard_map/pallas_call | solution.py:463
  21.2 0.2 collective-permute-start.10
  21.4 4.7 %collective-permute-start.8 = (f32[1,16,8,256]{3,2,1,0:T(8,128)S(1)}, f32[1,16,8,256]{3,2,1,0:T(8,128)S(1)}, u32[]{:S(2)}, u32[]{:S(2)}) collective-permute-start(f32[1,16,8,256]{3,2,1,0:T(8,128)S(1)} %get-tuple-element.54), channel_id=1, source_target_pairs={{0,1},{4,5},{2,3},{6,7},{1,0},{5,4},{3,2},{7,6},{8,9},{12,13},{10,... | collective-permute-start | bytes 393224 | tf_op jit(solution)/shard_map/ppermute | solution.py:491
  26.1 2.1 %shard_map.143 = (f32[2,16,32,256]{3,2,1,0:T(8,128)S(1)}, f32[2,16,32,128]{3,2,1,0:T(8,128)S(1)}, f32[2,16,32,256]{3,2,1,0:T(8,128)}) custom-call(s32[2]{0:T(128)S(1)} %copy-done.6, s32[2]{0:T(128)S(1)} %copy-done.8, f32[2,128]{1,0:T(2,128)S(1)} %copy-done.7, f32[2,16,32,256]{3,2,1,0:T(8,128)S(1)} %get-tuple-element.40.u, f32[2,16,32,256]{3,2,1,0:T(8,128)S(1)} %copy-done.5, ...), custom_call_target="tpu_custom_call" | custom-call | flops 8388608 | bytes 8388608 | tf_op jit(solution)/shard_map/pallas_call | solution.py:463
  28.2 0.2 collective-permute-start.9
  28.4 0.8 %shard_map.144 = (f32[2,16,32,256]{3,2,1,0:T(8,128)S(1)}, f32[2,16,32,128]{3,2,1,0:T(8,128)S(1)}, f32[16,16,128]{2,1,0:T(8,128)S(1)}, f32[16,16,128]{2,1,0:T(8,1...) custom-call(f32[1,16,8,256]{3,2,1,0:T(8,128)S(1)} %collective-permut, ...), custom_call_target="tpu_custom_call", output_to_operand_aliasing={{0}: (5, {}), {1}: (6, {})} | custom-call | flops 1048576 | bytes 1048576 | tf_op jit(solution)/shard_map/pallas_call | solution.py:463
  29.2 2.5 %collective-permute-start.11 = (f32[16,16,128]{2,1,0:T(8,128)S(1)}, f32[16,16,128]{2,1,0:T(8,128)S(1)}, u32[]{:S(2)}, u32[]{:S(2)}) collective-permute-start(f32[16,16,128]{2,1,0:T(8,128)S(1)} %get-tuple-element.60), channel_id=1, source_target_pairs={{0,24},{8,16},{16,8},{24,0},{1,25},{9,17},{17,9},{25,1},{2,26},{10... | collective-permute-start | bytes 393224 | tf_op jit(solution)/shard_map/ppermute | solution.py:579
  31.8 0.5 %collective-permute-start.12 = (f32[16,16,128]{2,1,0:T(8,128)S(1)}, f32[16,16,128]{2,1,0:T(8,128)S(1)}, u32[]{:S(2)}, u32[]{:S(2)}) collective-permute-start(f32[16,16,128]{2,1,0:T(8,128)S(1)} %get-tuple-element.61), channel_id=1, source_target_pairs={{0,8},{8,0},{16,24},{24,16},{1,9},{9,1},{17,25},{25,17},{2,10},{10... | collective-permute-start | bytes 393224 | tf_op jit(solution)/shard_map/ppermute | solution.py:579
  32.3 0.5 %collective-permute-start.13 = (f32[16,16,128]{2,1,0:T(8,128)S(1)}, f32[16,16,128]{2,1,0:T(8,128)S(1)}, u32[]{:S(2)}, u32[]{:S(2)}) collective-permute-start(f32[16,16,128]{2,1,0:T(8,128)S(1)} %get-tuple-element.62), channel_id=1, source_target_pairs={{0,16},{8,24},{16,0},{24,8},{1,17},{9,25},{17,1},{25,9},{2,18},{10... | collective-permute-start | bytes 393224 | tf_op jit(solution)/shard_map/ppermute | solution.py:579
  32.8 2.7 %shard_map.145 = (f32[2,16,32,256]{3,2,1,0:T(8,128)S(1)}, f32[2,16,32,256]{3,2,1,0:T(8,128)}, f32[2,16,32,256]{3,2,1,0:T(8,128)}) custom-call(s32[2]{0:T(128)S(1)} %copy-done.6, s32[2,1024]{1,0:T(2,128)} %rec_hbm.3, f32[2,128,1024]{2,1,0:T(8,128)} %trace_hbm.3, f32[2,16,32,256]{3,2,1,0:T(8,128)S(1)} %get-tuple-element.43.a.refs_3_, ...), custom_call_target="tpu_custom_call" | custom-call | flops 8388608 | bytes 8388608 | tf_op jit(solution)/shard_map/pallas_call | solution.py:463
  35.5 1.3 %shard_map.146 = (f32[2,16,32,256]{3,2,1,0:T(8,128)S(1)}, f32[2,16,32,256]{3,2,1,0:T(8,128)}) custom-call(f32[1,16,8,256]{3,2,1,0:T(8,128)S(1)} %collective-permute-done.8.refs_0_, f32[1,16,8,256]{3,2,1,0:T(8,128)S(1)} %collective-permute-done.9.refs_1_, f32[1,2,4,32,256]{4,3,2,1,0:T(8,128)S(1)} %collective-permute-done.10.refs_2_, ...), custom_call_target="tpu_custom_call", output_to_operand_aliasing={{0}: (4, {})} | custom-call | flops 1048576 | bytes 1048576 | tf_op jit(solution)/shard_map/pallas_call | solution.py:463
  36.8 2.1 %collective-permute-done.12.second = f32[16,16,128]{2,1,0:T(8,128)S(1)} collective-permute-done((f32[16,16,128]{2,1,0:T(8,128)S(1)}, f32[16,16,128]{2,1,0:T(8,128)S(1)}, u32[]{:S(2)}, u32[]{:S(2)}) %collective-permute-start.12) | collective-permute-done | bytes 131104 | tf_op jit(solution)/shard_map/ppermute | solution.py:579
  38.9 1.4 %shard_map.147 = f32[16,32,64]{2,1,0:T(8,128)} custom-call(f32[16,32,256]{2,1,0:T(8,128)S(1)} %copy-done.1, f32[16,16,128]{2,1,0:T(8,128)S(1)} %get-tuple-element.59.own, f32[16,16,128]{2,1,0:T(8,128)S(1)} %collective-permute-done.11.first, f32[16,16,128]{2,1,0:T(8,128)S(1)} %collective-permute-done.12.second, f32[16,16,128]{2,1,0:T(8,128)S(1)} %collective-permute-done.13.third), custom_call_target="tpu_custom_call" | custom-call | flops 1048576 | bytes 1048576 | tf_op jit(solution)/shard_map/pallas_call | solution.py:463
  (25 shorter events, 0.1 us)
Async XLA Ops:
  0.6 1.0 %copy-start = (f32[16,32,256]{2,1,0:T(8,128)S(1)}, f32[16,32,256]{2,1,0:T(8,128)}, u32[]{:S(2)}) copy-start(f32[16,32,256]{2,1,0:T(8,128)} %cour.11) | copy-start | bytes 1572868
  1.7 1.2 %copy-start.2 = (f32[2,16,32,256]{3,2,1,0:T(8,128)S(1)}, f32[2,16,32,256]{3,2,1,0:T(8,128)}, u32[]{:S(2)}) copy-start(f32[2,16,32,256]{3,2,1,0:T(8,128)} %a_old.3) | copy-start | bytes 3145732
  2.9 1.2 %copy-start.4 = (f32[2,16,32,256]{3,2,1,0:T(8,128)S(1)}, f32[2,16,32,256]{3,2,1,0:T(8,128)}, u32[]{:S(2)}) copy-start(f32[2,16,32,256]{3,2,1,0:T(8,128)} %u_old.3) | copy-start | bytes 3145732
  4.2 8.0 %copy-start.1 = (f32[16,32,256]{2,1,0:T(8,128)S(1)}, f32[16,32,256]{2,1,0:T(8,128)}, u32[]{:S(2)}) copy-start(f32[16,32,256]{2,1,0:T(8,128)} %cour.11) | copy-start | bytes 1572868
  4.2 8.0 %copy-start.3 = (f32[2,16,32,256]{3,2,1,0:T(8,128)S(1)}, f32[2,16,32,256]{3,2,1,0:T(8,128)}, u32[]{:S(2)}) copy-start(f32[2,16,32,256]{3,2,1,0:T(8,128)} %a_old.3) | copy-start | bytes 3145732
  4.2 8.0 %copy-start.5 = (f32[2,16,32,256]{3,2,1,0:T(8,128)S(1)}, f32[2,16,32,256]{3,2,1,0:T(8,128)}, u32[]{:S(2)}) copy-start(f32[2,16,32,256]{3,2,1,0:T(8,128)} %u_old.3) | copy-start | bytes 3145732
  4.2 14.3 %collective-permute-start.2 = (f32[2,2,4,32,256]{4,3,2,1,0:T(8,128)S(1)}, f32[2,2,4,32,256]{4,3,2,1,0:T(8,128)S(1)}, u32[]{:S(2)}, u32[]{:S(2)}) collective-permute-start(f32[2,2,4,32,256]{4,3,2,1,0:T(8,128)S(1)} %shard_map.138), channel_id=1, source_target_pairs={{0,4},{1,5},{2,6},{3,7},{4,0},{5,1},{6,2},{7,3},{8,12},{9,13},{10,... | collective-permute-start | bytes 1572872 | tf_op jit(solution)/shard_map/ppermute | solution.py:491
  6.4 12.1 %collective-permute-start = (f32[1,16,8,256]{3,2,1,0:T(8,128)S(1)}, f32[1,16,8,256]{3,2,1,0:T(8,128)S(1)}, u32[]{:S(2)}, u32[]{:S(2)}) collective-permute-start(f32[1,16,8,256]{3,2,1,0:T(8,128)S(1)} %get-tuple-element.34), channel_id=1, source_target_pairs={{0,1},{4,5},{2,3},{6,7},{1,0},{5,4},{3,2},{7,6},{8,9},{12,13},{10,... | collective-permute-start | bytes 393224 | tf_op jit(solution)/shard_map/ppermute | solution.py:491
  9.0 3.2 %copy-start.8 = (s32[2]{0:T(128)S(1)}, s32[2]{0:T(128)}, u32[]{:S(2)}) copy-start(s32[2]{0:T(128)} %src_ref.3) | copy-start | bytes 28
  9.0 3.2 %copy-start.6 = (s32[2]{0:T(128)S(1)}, s32[2]{0:T(128)}, u32[]{:S(2)}) copy-start(s32[2]{0:T(128)} %step_ref.7) | copy-start | bytes 28
  9.0 3.2 %copy-start.7 = (f32[2,128]{1,0:T(2,128)S(1)}, f32[2,128]{1,0:T(2,128)}, u32[]{:S(2)}) copy-start(f32[2,128]{1,0:T(2,128)} %wave_ref.3) | copy-start | bytes 3076
  9.0 9.5 %collective-permute-start.1 = (f32[1,16,8,256]{3,2,1,0:T(8,128)S(1)}, f32[1,16,8,256]{3,2,1,0:T(8,128)S(1)}, u32[]{:S(2)}, u32[]{:S(2)}) collective-permute-start(f32[1,16,8,256]{3,2,1,0:T(8,128)S(1)} %get-tuple-element.35), channel_id=1, source_target_pairs={{1,2},{5,6},{2,1},{6,5},{0,4},{4,0},{3,7},{7,3},{9,10},{13,14},{10... | collective-permute-start | bytes 393224 | tf_op jit(solution)/shard_map/ppermute | solution.py:491
  9.1 10.7 %collective-permute-start.3 = (f32[1,16,8,256]{3,2,1,0:T(8,128)S(1)}, f32[1,16,8,256]{3,2,1,0:T(8,128)S(1)}, u32[]{:S(2)}, u32[]{:S(2)}) collective-permute-start(f32[1,16,8,256]{3,2,1,0:T(8,128)S(1)} %get-tuple-element.41), channel_id=1, source_target_pairs={{0,1},{4,5},{2,3},{6,7},{1,0},{5,4},{3,2},{7,6},{8,9},{12,13},{10,... | collective-permute-start | bytes 393224 | tf_op jit(solution)/shard_map/ppermute | solution.py:491
  19.0 9.5 %collective-permute-start.7 = (f32[1,2,4,32,256]{4,3,2,1,0:T(8,128)S(1)}, f32[1,2,4,32,256]{4,3,2,1,0:T(8,128)S(1)}, u32[]{:S(2)}, u32[]{:S(2)}) collective-permute-start(f32[1,2,4,32,256]{4,3,2,1,0:T(8,128)S(1)} %get-tuple-element.48), channel_id=1, source_target_pairs={{0,4},{1,5},{2,6},{3,7},{4,0},{5,1},{6,2},{7,3},{8,12},{9,13},{10,... | collective-permute-start | bytes 786440 | tf_op jit(solution)/shard_map/ppermute | solution.py:491
  19.0 1.7 %collective-permute-start.4 = (f32[1,16,8,256]{3,2,1,0:T(8,128)S(1)}, f32[1,16,8,256]{3,2,1,0:T(8,128)S(1)}, u32[]{:S(2)}, u32[]{:S(2)}) collective-permute-start(f32[1,16,8,256]{3,2,1,0:T(8,128)S(1)} %get-tuple-element.42), channel_id=1, source_target_pairs={{1,2},{5,6},{2,1},{6,5},{0,4},{4,0},{3,7},{7,3},{9,10},{13,14},{10... | collective-permute-start | bytes 393224 | tf_op jit(solution)/shard_map/ppermute | solution.py:491
  19.5 8.7 %collective-permute-start.5 = (f32[1,16,8,256]{3,2,1,0:T(8,128)S(1)}, f32[1,16,8,256]{3,2,1,0:T(8,128)S(1)}, u32[]{:S(2)}, u32[]{:S(2)}) collective-permute-start(f32[1,16,8,256]{3,2,1,0:T(8,128)S(1)} %get-tuple-element.46), channel_id=1, source_target_pairs={{0,1},{4,5},{2,3},{6,7},{1,0},{5,4},{3,2},{7,6},{8,9},{12,13},{10,... | collective-permute-start | bytes 393224 | tf_op jit(solution)/shard_map/ppermute | solution.py:491
  19.8 8.6 %collective-permute-start.6 = (f32[1,16,8,256]{3,2,1,0:T(8,128)S(1)}, f32[1,16,8,256]{3,2,1,0:T(8,128)S(1)}, u32[]{:S(2)}, u32[]{:S(2)}) collective-permute-start(f32[1,16,8,256]{3,2,1,0:T(8,128)S(1)} %get-tuple-element.47), channel_id=1, source_target_pairs={{1,2},{5,6},{2,1},{6,5},{0,4},{4,0},{3,7},{7,3},{9,10},{13,14},{10... | collective-permute-start | bytes 393224 | tf_op jit(solution)/shard_map/ppermute | solution.py:491
  21.2 14.3 %collective-permute-start.10 = (f32[1,2,4,32,256]{4,3,2,1,0:T(8,128)S(1)}, f32[1,2,4,32,256]{4,3,2,1,0:T(8,128)S(1)}, u32[]{:S(2)}, u32[]{:S(2)}) collective-permute-start(f32[1,2,4,32,256]{4,3,2,1,0:T(8,128)S(1)} %get-tuple-element.56), channel_id=1, source_target_pairs={{0,4},{1,5},{2,6},{3,7},{4,0},{5,1},{6,2},{7,3},{8,12},{9,13},{10,... | collective-permute-start | bytes 786440 | tf_op jit(solution)/shard_map/ppermute | solution.py:491
  21.4 10.9 %collective-permute-start.8 = (f32[1,16,8,256]{3,2,1,0:T(8,128)S(1)}, f32[1,16,8,256]{3,2,1,0:T(8,128)S(1)}, u32[]{:S(2)}, u32[]{:S(2)}) collective-permute-start(f32[1,16,8,256]{3,2,1,0:T(8,128)S(1)} %get-tuple-element.54), channel_id=1, source_target_pairs={{0,1},{4,5},{2,3},{6,7},{1,0},{5,4},{3,2},{7,6},{8,9},{12,13},{10,... | collective-permute-start | bytes 393224 | tf_op jit(solution)/shard_map/ppermute | solution.py:491
  28.2 7.3 %collective-permute-start.9 = (f32[1,16,8,256]{3,2,1,0:T(8,128)S(1)}, f32[1,16,8,256]{3,2,1,0:T(8,128)S(1)}, u32[]{:S(2)}, u32[]{:S(2)}) collective-permute-start(f32[1,16,8,256]{3,2,1,0:T(8,128)S(1)} %get-tuple-element.55), channel_id=1, source_target_pairs={{1,2},{5,6},{2,1},{6,5},{0,4},{4,0},{3,7},{7,3},{9,10},{13,14},{10... | collective-permute-start | bytes 393224 | tf_op jit(solution)/shard_map/ppermute | solution.py:491
  29.2 7.6 %collective-permute-start.11 = (f32[16,16,128]{2,1,0:T(8,128)S(1)}, f32[16,16,128]{2,1,0:T(8,128)S(1)}, u32[]{:S(2)}, u32[]{:S(2)}) collective-permute-start(f32[16,16,128]{2,1,0:T(8,128)S(1)} %get-tuple-element.60), channel_id=1, source_target_pairs={{0,24},{8,16},{16,8},{24,0},{1,25},{9,17},{17,9},{25,1},{2,26},{10... | collective-permute-start | bytes 393224 | tf_op jit(solution)/shard_map/ppermute | solution.py:579
  31.8 7.1 %collective-permute-start.12 = (f32[16,16,128]{2,1,0:T(8,128)S(1)}, f32[16,16,128]{2,1,0:T(8,128)S(1)}, u32[]{:S(2)}, u32[]{:S(2)}) collective-permute-start(f32[16,16,128]{2,1,0:T(8,128)S(1)} %get-tuple-element.61), channel_id=1, source_target_pairs={{0,8},{8,0},{16,24},{24,16},{1,9},{9,1},{17,25},{25,17},{2,10},{10... | collective-permute-start | bytes 393224 | tf_op jit(solution)/shard_map/ppermute | solution.py:579
  32.3 6.6 %collective-permute-start.13 = (f32[16,16,128]{2,1,0:T(8,128)S(1)}, f32[16,16,128]{2,1,0:T(8,128)S(1)}, u32[]{:S(2)}, u32[]{:S(2)}) collective-permute-start(f32[16,16,128]{2,1,0:T(8,128)S(1)} %get-tuple-element.62), channel_id=1, source_target_pairs={{0,16},{8,24},{16,0},{24,8},{1,17},{9,25},{17,1},{25,9},{2,18},{10... | collective-permute-start | bytes 393224 | tf_op jit(solution)/shard_map/ppermute | solution.py:579
